TPU v7x, 512 devices: a whole 4x8x8 slice. The times are simulated.
512 devices in a mesh: pipe: 32 (over x, z), expert: 16 (over y, core).
Axes of the slice: x: 4, y: 8, z: 8, core: 2. Of those that a mesh axis runs over, the one named last changes fastest.
Arguments:
- upstream: bfloat16 [32, 1024, 7168], P('pipe', None, 'expert'), may hold values from -6 to 6
- shared_down: bfloat16 [32, 1024, 7168], P('pipe', None, 'expert'), may hold values from -0.0625 to 0.0625
- shared_gate: bfloat16 [32, 7168, 1024], P('pipe', 'expert'), may hold values from -0.1875 to 0.1875
- shared_up: bfloat16 [32, 7168, 1024], P('pipe', 'expert'), may hold values from -0.1875 to 0.1875
- router_weight: bfloat16 [32, 7168, 256], P('pipe', 'expert'), may hold values from -2 to 2
- gate_pre: bfloat16 [32, 1024, 1024], P('pipe', 'expert'), may hold values from -6 to 6
- up_pre: bfloat16 [32, 1024, 1024], P('pipe', 'expert'), may hold values from -6 to 6
- gate_grad: float32 [32, 1024, 8], P('pipe'), may hold values from -6 to 6
- gate_scores: float32 [32, 1024, 8], P('pipe'), may hold values from 0.05 to 0.95
- expert_ids: int32 [32, 1024, 8], P('pipe'), may hold values from 0 to 255, all different within a row
Outputs:
- down_grad: bfloat16 [32, 1024, 7168], P('pipe', None, 'expert')
Inputs may be any that keep to these rules, and one draw needn't show every extreme that they name: `expert_ids`: each token names 8 different experts.
All inputs are finite; a program needn't handle non-finite values.
Results may differ from a plain program's by a relative error of at most 0.02.
Values may be sent and summed in bfloat16 or wider, within the bound.
A program may use at most 64 MiB of HBM per device.

v0:
```python
import jax
import jax.numpy as jnp
from jax import lax
from jax.sharding import PartitionSpec as P


def passed_along(x, axis, by):
    length = lax.axis_size(axis)
    return lax.ppermute(x, axis, [(i, (i + by) % length) for i in range(length)])


def contract_last(left, right):
    return lax.dot_general(
        left, right, (((1,), (1,)), ((), ())), preferred_element_type=jnp.float32
    )


def section_backward(
    incoming, w_down, w_gate, w_up, w_router, pre_gate, pre_up, grad_gate, scores, chosen
):
    hid_width = w_down.shape[0]
    hidden_grad = lax.psum_scatter(
        contract_last(incoming, w_down)
        .astype(jnp.bfloat16)
        .astype(jnp.float32)
        .astype(jnp.bfloat16),
        "expert",
        scatter_dimension=0,
        tiled=True,
    ).astype(jnp.float32)
    act_a = pre_gate.astype(jnp.float32)
    act_b = pre_up.astype(jnp.float32)
    sigma = jax.nn.sigmoid(act_a)
    gate_part = (hidden_grad * act_b * sigma * (1.0 + act_a * (1.0 - sigma))).astype(jnp.bfloat16)
    up_part = (hidden_grad * act_a * sigma).astype(jnp.bfloat16)
    stacked = jnp.concatenate([gate_part, up_part], axis=1)
    piece = lax.all_gather(stacked, "expert", axis=0, tiled=True)
    shared_term = contract_last(piece[:, :hid_width], w_gate) + contract_last(
        piece[:, hid_width:], w_up
    )
    total = jnp.sum(scores, axis=-1, keepdims=True)
    mixed = jnp.sum(grad_gate * scores, axis=-1, keepdims=True)
    logit_grad = 2.5 * (grad_gate - mixed / total) / total * scores * (1.0 - scores)
    n_experts = w_router.shape[1]
    columns = lax.broadcasted_iota(jnp.int32, (1, n_experts), 1)
    dense = jnp.zeros((grad_gate.shape[0], n_experts), jnp.float32)
    for slot in range(grad_gate.shape[1]):
        dense = dense + jnp.where(
            chosen[:, slot : slot + 1] == columns, logit_grad[:, slot : slot + 1], 0.0
        )
    dense_grad = dense.astype(jnp.bfloat16)
    router_term = contract_last(dense_grad, w_router)
    return (shared_term + router_term).astype(jnp.bfloat16)


def shards(
    upstream,
    shared_down,
    shared_gate,
    shared_up,
    router_weight,
    gate_pre,
    up_pre,
    gate_grad,
    gate_scores,
    expert_ids,
):
    incoming = passed_along(upstream, "pipe", -1)
    local_grad = section_backward(
        incoming[0],
        shared_down[0],
        shared_gate[0],
        shared_up[0],
        router_weight[0],
        gate_pre[0],
        up_pre[0],
        gate_grad[0],
        gate_scores[0],
        expert_ids[0],
    )
    return passed_along(local_grad[None], "pipe", -1)


def solution(mesh):
    in_specs = (
        P("pipe", None, "expert"),
        P("pipe", None, "expert"),
        P("pipe", "expert", None),
        P("pipe", "expert", None),
        P("pipe", "expert", None),
        P("pipe", "expert", None),
        P("pipe", "expert", None),
        P("pipe", None, None),
        P("pipe", None, None),
        P("pipe", None, None),
    )
    out_specs = P("pipe", None, "expert")
    return jax.shard_map(shards, mesh=mesh, in_specs=in_specs, out_specs=out_specs, check_vma=False)
```

profile of v0, /device:TPU:1, one launch (start us, length us, event | category | flops | bytes accessed | tf_op | source)
XLA Modules:
  0.0 193.9 jit_solution(15311759996516569010)
XLA Ops:
  6.5 0.0 copy-start
  6.5 0.0 reduce-scatter.2.cloned.1.call-start
  6.5 13.8 %collective-permute-start = (bf16[1,1024,448]{1,2,0:T(8,128)(2,1)}, bf16[1,1024,448]{1,2,0:T(8,128)(2,1)S(1)}, u32[]{:S(2)}, u32[]{:S(2)}) collective-permute-start(bf16[1,1024,448]{1,2,0:T(8,128)(2,1)} %param.10), channel_id=1, source_target_pairs={{0,496},{16,0},{32,16},{48,32},{64,48},{80,64},{96,80},{112,96},{1... | collective-permute-start | bytes 2752520 | tf_op jit(solution)/shard_map/ppermute | solution.py:9
  20.3 19.3 %collective-permute-done = bf16[1,1024,448]{1,2,0:T(8,128)(2,1)S(1)} collective-permute-done((bf16[1,1024,448]{1,2,0:T(8,128)(2,1)}, bf16[1,1024,448]{1,2,0:T(8,128)(2,1)S(1)}, u32[]{:S(2)}, u32[]{:S(2)}) %collective-permute-start) | collective-permute-done | bytes 917536 | tf_op jit(solution)/shard_map/ppermute | solution.py:9
  39.7 0.0 copy-done
  39.7 2.6 %convolution_convert_fusion = bf16[1024,1024]{1,0:T(8,128)(2,1)} fusion(bf16[1,1024,448]{1,2,0:T(8,128)(2,1)S(1)} %copy-done, bf16[1,1024,448]{1,2,0:T(8,128)(2,1)S(1)} %collective-permute-done), kind=kOutput, calls=%fused_computation.4 | convolution fusion | flops 940572672 | bytes 3932160 | tf_op jit(solution)/shard_map/dot_general | solution.py:13
  42.3 0.0 copy-start.2
  42.3 0.0 copy-start.3
  42.3 0.0 copy-start.1
  42.3 0.0 copy-start.4
  42.3 0.0 copy-start.5
  42.3 0.0 copy-start.7
  42.3 0.0 reduce-scatter.2.cloned.1.call-update
  42.4 0.0 all-gather.2.cloned.1.call-start
  42.4 60.4 %reduce-scatter.2.cloned.1.call-done = bf16[64,1024]{1,0:T(8,128)(2,1)} async-done(((bf16[1024,1024]{1,0:T(8,128)(2,1)}), bf16[64,1024]{1,0:T(8,128)(2,1)}) %reduce-scatter.2.cloned.1.call-update) | async-done | bytes 131088 | tf_op jit(solution)/shard_map/reduce_scatter | solution.py:22
  102.8 0.0 copy-done.2
  102.8 0.0 copy-done.3
  102.8 1.0 fusion.28
  103.9 0.7 pad_maximum_fusion
  104.6 0.0 all-gather.2.cloned.1.call-update
  104.6 0.0 copy-done.1
  104.7 0.0 copy-done.4
  104.8 0.0 copy-done.5
  104.8 0.0 copy-start.8
  104.8 45.7 %all-gather.2.cloned.1.call-done = bf16[1024,2048]{1,0:T(8,128)(2,1)} async-done(((bf16[64,2048]{1,0:T(8,128)(2,1)}), bf16[1024,2048]{1,0:T(8,128)(2,1)}) %all-gather.2.cloned.1.call-update) | async-done | bytes 4194320 | tf_op jit(solution)/shard_map/all_gather | solution.py:37
  150.5 0.0 copy-done.7
  150.5 0.0 copy-start.6
  150.5 2.9 %fusion.2 = f32[1024,448]{0,1:T(8,128)S(1)} fusion(bf16[1024,2048]{1,0:T(8,128)(2,1)} %all-gather.2.cloned.1.call-done, bf16[1,448,1024]{2,1,0:T(8,128)(2,1)S(1)} %copy-done.7), kind=kOutput, calls=%fused_computation.2 | convolution fusion | flops 939524096 | bytes 4849664 | tf_op jit(solution)/shard_map/dot_general | solution.py:13
  153.4 0.0 copy-done.8
  153.4 0.0 copy-done.6
  153.4 0.0 copy-start.9
  153.4 1.2 fusion
  154.6 0.0 copy-done.9
  154.6 4.4 %fusion.4 = bf16[1,1024,448]{1,2,0:T(8,128)(2,1)S(1)} fusion(f32[1024,448]{0,1:T(8,128)S(1)} %fusion.2, f32[1024,448]{0,1:T(8,128)S(1)} %fusion, f32[1024]{0:T(1024)S(1)} %bitcast.62, s32[1024]{0:T(1024)S(1)} %bitcast.70, f32[1024]{0:T(1024)S(1)} %bitcast.63, s32[1024]{0:T(1024)S(1)} %bitcast.71, f32[1024]{0:T(1024)S(1)} %bitcast.64, s32[1024]{0:T(1024)S(1)} %bitcast.72, ...), kind=kOutput, calls=%fused_computation.6 | convolution fusion | flops 242548736 | bytes 4882432 | tf_op jit(solution)/shard_map/dot_general | solution.py:13
  159.0 7.7 %collective-permute-start.1 = (bf16[1,1024,448]{1,2,0:T(8,128)(2,1)S(1)}, bf16[1,1024,448]{1,2,0:T(8,128)(2,1)S(1)}, u32[]{:S(2)}, u32[]{:S(2)}) collective-permute-start(bf16[1,1024,448]{1,2,0:T(8,128)(2,1)S(1)} %fusion.4), channel_id=1, source_target_pairs={{0,496},{16,0},{32,16},{48,32},{64,48},{80,64},{96,80},{112,96},{1... | collective-permute-start | bytes 2752520 | tf_op jit(solution)/shard_map/ppermute | solution.py:9
  166.7 19.4 %collective-permute-done.1 = bf16[1,1024,448]{1,2,0:T(8,128)(2,1)S(1)} collective-permute-done((bf16[1,1024,448]{1,2,0:T(8,128)(2,1)S(1)}, bf16[1,1024,448]{1,2,0:T(8,128)(2,1)S(1)}, u32[]{:S(2)}, u32[]{:S(2)}) %collective-permute-start.1) | collective-permute-done | bytes 917536 | tf_op jit(solution)/shard_map/ppermute | solution.py:9
  186.1 0.9 copy.12
  (6 shorter events, 0.1 us)
Async XLA Ops:
  6.5 33.1 %copy-start = (bf16[1,1024,448]{1,2,0:T(8,128)(2,1)S(1)}, bf16[1,1024,448]{1,2,0:T(8,128)(2,1)}, u32[]{:S(2)}) copy-start(bf16[1,1024,448]{1,2,0:T(8,128)(2,1)} %param.11) | copy-start | bytes 2752516
  6.5 96.3 %reduce-scatter.2.cloned.1.call-start = ((), (), s32[]{:S(2)}) async-start(), calls=%async_computation.1 | async-start | bytes 2228224 | tf_op jit(solution)/shard_map/reduce_scatter | solution.py:22
  6.5 33.1 %collective-permute-start = (bf16[1,1024,448]{1,2,0:T(8,128)(2,1)}, bf16[1,1024,448]{1,2,0:T(8,128)(2,1)S(1)}, u32[]{:S(2)}, u32[]{:S(2)}) collective-permute-start(bf16[1,1024,448]{1,2,0:T(8,128)(2,1)} %param.10), channel_id=1, source_target_pairs={{0,496},{16,0},{32,16},{48,32},{64,48},{80,64},{96,80},{112,96},{1... | collective-permute-start | bytes 2752520 | tf_op jit(solution)/shard_map/ppermute | solution.py:9
  42.3 60.5 %copy-start.2 = (bf16[1,64,1024]{2,1,0:T(8,128)(2,1)S(1)}, bf16[1,64,1024]{2,1,0:T(8,128)(2,1)}, u32[]{:S(2)}) copy-start(bf16[1,64,1024]{2,1,0:T(8,128)(2,1)} %param.16) | copy-start | bytes 393220
  42.3 60.5 %copy-start.3 = (bf16[1,64,1024]{2,1,0:T(8,128)(2,1)S(1)}, bf16[1,64,1024]{2,1,0:T(8,128)(2,1)}, u32[]{:S(2)}) copy-start(bf16[1,64,1024]{2,1,0:T(8,128)(2,1)} %param.15) | copy-start | bytes 393220
  42.3 62.3 %copy-start.1 = (f32[1,1024,8]{1,2,0:T(8,128)S(1)}, f32[1,1024,8]{1,2,0:T(8,128)}, u32[]{:S(2)}) copy-start(f32[1,1024,8]{1,2,0:T(8,128)} %param.18) | copy-start | bytes 98308
  42.3 62.3 %copy-start.4 = (f32[1,1024,8]{1,2,0:T(8,128)S(1)}, f32[1,1024,8]{1,2,0:T(8,128)}, u32[]{:S(2)}) copy-start(f32[1,1024,8]{1,2,0:T(8,128)} %param.17) | copy-start | bytes 98308
  42.3 62.4 %copy-start.5 = (s32[1,1024,8]{1,2,0:T(8,128)S(1)}, s32[1,1024,8]{1,2,0:T(8,128)}, u32[]{:S(2)}) copy-start(s32[1,1024,8]{1,2,0:T(8,128)} %param.19) | copy-start | bytes 98308
  42.3 108.2 %copy-start.7 = (bf16[1,448,1024]{2,1,0:T(8,128)(2,1)S(1)}, bf16[1,448,1024]{2,1,0:T(8,128)(2,1)}, u32[]{:S(2)}) copy-start(bf16[1,448,1024]{2,1,0:T(8,128)(2,1)} %param.12) | copy-start | bytes 2752516
  42.4 108.1 %all-gather.2.cloned.1.call-start = ((), (), s32[]{:S(2)}) async-start(), calls=%async_computation.2 | async-start | bytes 4456448 | tf_op jit(solution)/shard_map/all_gather | solution.py:37
  104.8 48.6 %copy-start.8 = (bf16[1,448,1024]{2,1,0:T(8,128)(2,1)S(1)}, bf16[1,448,1024]{2,1,0:T(8,128)(2,1)}, u32[]{:S(2)}) copy-start(bf16[1,448,1024]{2,1,0:T(8,128)(2,1)} %param.13) | copy-start | bytes 2752516
  150.5 2.9 %copy-start.6 = (bf16[1024,2048]{1,0:T(8,128)(2,1)S(1)}, bf16[1024,2048]{1,0:T(8,128)(2,1)}, u32[]{:S(2)}) copy-start(bf16[1024,2048]{1,0:T(8,128)(2,1)} %all-gather.2.cloned.1.call-done) | copy-start | bytes 12582916
  153.4 1.2 copy-start.9
  159.0 27.1 %collective-permute-start.1 = (bf16[1,1024,448]{1,2,0:T(8,128)(2,1)S(1)}, bf16[1,1024,448]{1,2,0:T(8,128)(2,1)S(1)}, u32[]{:S(2)}, u32[]{:S(2)}) collective-permute-start(bf16[1,1024,448]{1,2,0:T(8,128)(2,1)S(1)} %fusion.4), channel_id=1, source_target_pairs={{0,496},{16,0},{32,16},{48,32},{64,48},{80,64},{96,80},{112,96},{1... | collective-permute-start | bytes 2752520 | tf_op jit(solution)/shard_map/ppermute | solution.py:9
Sparse Core Ops, SparseCore 0:
  42.5 60.2 reduce-scatter.1
  104.9 45.4 all-gather.1
where the time goes:
time: 194 us
  waiting for transfers between devices  145 us (75%)
  starting transfers between devices  21.6 us (11%)
  between operations  13.6 us (7%)
  matrix products  11.1 us (6%)
    reduce_scatter x1, waiting for transfers between devices, section_backward(): lax.psum_scatter(contract_last(incoming, w_down).astype(jnp.bfloat16).ast...  60.4 us
    all_gather x1, waiting for transfers between devices, section_backward(): piece = lax.all_gather(stacked, 'expert', axis=0, tiled=True)  45.7 us
    ppermute x2, waiting for transfers between devices, passed_along(): lax.ppermute(x, axis, [(i, (i + by) % length) for i in range(length)])  38.7 us
    ppermute x2, starting transfers between devices, passed_along(): lax.ppermute(x, axis, [(i, (i + by) % length) for i in range(length)])  21.5 us
    dot_general x4, matrix products, contract_last(): lax.dot_general(left, right, (((1,), (1,)), ((), ())), preferred_element_...  11.1 us
  transfers between devices with their start and end apart: 4, of which 4 were waited for; matrix products, arithmetic and copies ran while one was open for 0% of the time, Pallas kernels for 0%

commit v1 on v0

v1 whole, which is shorter than its diff:
```python
import functools

import jax
import jax.numpy as jnp
from jax import lax
from jax.experimental import pallas as pl
from jax.experimental.pallas import tpu as pltpu
from jax.sharding import PartitionSpec as P

MESH = pl.DeviceIdType.MESH
F32 = jnp.float32
BF16 = jnp.bfloat16
NEAR = (4, 2, -2, 0)
FAR = (3, -3, 1, -1)
ARRIVAL = ((0, 0), (1, 0), (1, 1), (0, 1), (0, 2), (1, 2), (1, 3), (0, 3))


def kernel(
    n_pipe, n_chip,
    up_ref, dn_ref, wg_ref, wu_ref, wr_ref, pa_ref, pb_ref, gg_ref, sc_ref, id_ref,
    out_ref,
    up, dn, wg, wu, wr, pa, pb, gg, sc, ids, c1, c2, pf, rbuf, sbuf, gbuf, rterm, obuf,
    loc_sem, a_send, a_recv, w_send, w_recv, rs_send, rs_recv, ag_send, ag_recv, d_send, d_recv,
):
    feat = up_ref.shape[0]
    tile = pa_ref.shape[0] * 2
    hid = pa_ref.shape[1]
    half = hid // 2
    p = lax.axis_index("pipe")
    e = lax.axis_index("expert")
    y, c = e // 2, e % 2
    role = lax.rem(c + y, 2)
    before = lax.rem(p + n_pipe - 1, n_pipe)
    after = lax.rem(p + 1, n_pipe)
    partner = (p, 2 * y + 1 - c)
    plus = (p, 2 * lax.rem(y + 1, n_chip) + c)
    minus = (p, 2 * lax.rem(y + n_chip - 1, n_chip) + c)
    near = role == 0
    far = role == 1

    def remote(src, dst, send, recv, device):
        return pltpu.make_async_remote_copy(
            src_ref=src, dst_ref=dst, send_sem=send, recv_sem=recv, device_id=device, device_id_type=MESH
        )

    def arrived(dst, recv):
        remote(dst, dst, recv, recv, partner).wait_recv()

    def sent(src, send):
        remote(src, src, send, send, partner).wait_send()

    barrier = pltpu.get_barrier_semaphore()
    for device in ((after, 2 * y), (after, 2 * y + 1), partner, plus, minus):
        pl.semaphore_signal(barrier, inc=1, device_id=device, device_id_type=MESH)

    mine = pl.ds(pl.multiple_of(c * feat, feat), feat)
    mine_rows = pl.ds(pl.multiple_of(c * (tile // 2), tile // 2), tile // 2)
    wide = ((dn_ref, dn, mine), (wr_ref, wr, mine), (pa_ref, pa, mine_rows), (pb_ref, pb, mine_rows),
            (wg_ref, wg, mine), (wu_ref, wu, mine))
    local = [pltpu.make_async_copy(s, d, loc_sem.at[i]) for i, (s, d) in enumerate(((gg_ref, gg), (sc_ref, sc), (id_ref, ids)))]
    local += [pltpu.make_async_copy(s, d.at[rows], loc_sem.at[3 + i]) for i, (s, d, rows) in enumerate(wide)]
    for copy in local:
        copy.start()

    pl.semaphore_wait(barrier, 5)

    def lanes(distance):
        return pl.ds(pl.multiple_of(lax.rem(y + n_chip + distance, n_chip) * tile, tile), tile)

    incoming = []
    for i, (r, s) in enumerate(ARRIVAL):
        device = (before, 2 * y + lax.rem(y + r, 2))
        copy = remote(up_ref.at[:, lanes((NEAR, FAR)[r][s])], up.at[s, mine], a_send.at[i], a_recv.at[s, c], device)
        copy.start()
        incoming.append(copy)
    exchange = [remote(s, d.at[rows], w_send.at[i], w_recv.at[i], partner) for i, (s, d, rows) in enumerate(wide)]
    for copy in exchange:
        copy.start()

    theirs = pl.ds(pl.multiple_of((1 - c) * feat, feat), feat)
    theirs_rows = pl.ds(pl.multiple_of((1 - c) * (tile // 2), tile // 2), tile // 2)

    def have(i):
        rows = theirs_rows if i in (2, 3) else theirs
        local[3 + i].wait()
        arrived(wide[i][1].at[rows], w_recv.at[i])

    def tile_lanes(s):
        distance = jnp.where(near, NEAR[s], FAR[s])
        return pl.ds(pl.multiple_of(lax.rem(y + n_chip + distance, n_chip) * tile, tile), tile)

    for i in range(3):
        local[i].wait()
    have(1)
    for s in range(4):
        where = tile_lanes(s)
        grad, score, chosen = gg[:, where], sc[:, where], ids[:, where]
        total = jnp.sum(score, axis=0, keepdims=True)
        mixed = jnp.sum(grad * score, axis=0, keepdims=True)
        logit = 2.5 * (grad - mixed / total) / total * score * (1.0 - score)
        n_experts = wr.shape[1]
        rows = lax.broadcasted_iota(jnp.int32, (n_experts, tile), 0)
        dense = jnp.zeros((n_experts, tile), F32)
        for k in range(grad.shape[0]):
            dense = dense + jnp.where(chosen[k : k + 1] == rows, logit[k : k + 1], 0.0)
        rterm[s] = jnp.dot(wr[...], dense.astype(BF16), preferred_element_type=F32)

    have(2)
    have(3)

    @pl.when(near)
    def _():
        a, b = pa[...].astype(F32), pb[...].astype(F32)
        sigma = 1.0 / (1.0 + jnp.exp(-a))
        c1[...] = b * sigma * (1.0 + a * (1.0 - sigma))
        c2[...] = a * sigma

    have(0)

    def rs_copy(src, slot, device, send, cols=slice(None)):
        return remote(src.at[:, cols], rbuf.at[slot, :, cols], rs_send.at[send], rs_recv.at[slot], device)

    low, high = pl.ds(0, half), pl.ds(half, half)
    for s in range(4):
        for other in range(2):
            rows = pl.ds(other * feat, feat)
            arrived(up.at[s, rows], a_recv.at[s, other])
        pf[...] = lax.dot_general(up[s], dn[...], (((0,), (0,)), ((), ())), preferred_element_type=F32)

        @pl.when(near)
        def _(s=s):
            if s == 0:
                sbuf[0] = pf[...].astype(BF16)
                rs_copy(sbuf.at[0], 0, plus, 0, low).start()
                rs_copy(sbuf.at[0], 1, minus, 3, high).start()
            elif s < 3:
                arrived(rbuf.at[s - 1], rs_recv.at[s - 1])
                sbuf[s] = (pf[...] + rbuf[s - 1].astype(F32)).astype(BF16)
                rs_copy(sbuf.at[s], s + 1, (plus, minus)[s - 1], s).start()
            else:
                arrived(rbuf.at[2], rs_recv.at[2])
                arrived(rbuf.at[3], rs_recv.at[3])
                hidden = pf[...] + rbuf[2].astype(F32) + rbuf[3].astype(F32)
                gbuf[3, :, :hid] = (hidden * c1[...]).astype(BF16)
                gbuf[3, :, hid:] = (hidden * c2[...]).astype(BF16)

        @pl.when(far)
        def _(s=s):
            if s < 2:
                cols = (low, high)[s]
                arrived(rbuf.at[s, :, cols], rs_recv.at[s])
                if s == 0:
                    sbuf[s, :, :half] = (pf[:, :half] + rbuf[s, :, :half].astype(F32)).astype(BF16)
                    sbuf[s, :, half:] = pf[:, half:].astype(BF16)
                else:
                    sbuf[s, :, :half] = pf[:, :half].astype(BF16)
                    sbuf[s, :, half:] = (pf[:, half:] + rbuf[s, :, half:].astype(F32)).astype(BF16)
            else:
                arrived(rbuf.at[s], rs_recv.at[s])
                sbuf[s] = (pf[...] + rbuf[s].astype(F32)).astype(BF16)
            rs_copy(sbuf.at[s], s, (plus, minus)[s % 2], s).start()

    def ag_copy(here, there, device, send, recv, cols=slice(None)):
        return remote(gbuf.at[here, :, cols], gbuf.at[there, :, cols], ag_send.at[send], ag_recv.at[recv], device)

    gate_cols, up_cols = pl.ds(0, hid), pl.ds(hid, hid)

    have(4)
    have(5)

    @pl.when(near)
    def _():
        ag_copy(3, 3, plus, 0, 3).start()
        ag_copy(3, 2, minus, 1, 2).start()

    for s in (3, 2, 1, 0):

        @pl.when(near)
        def _(s=s):
            if s == 2:
                arrived(gbuf.at[2], ag_recv.at[2])
                ag_copy(2, 1, plus, 2, 1).start()
                arrived(gbuf.at[1], ag_recv.at[1])
                ag_copy(1, 0, minus, 3, 0).start()
            if s == 0:
                arrived(gbuf.at[0, :, gate_cols], ag_recv.at[0])
                arrived(gbuf.at[0, :, up_cols], ag_recv.at[4])

        @pl.when(far)
        def _(s=s):
            if s == 3:
                arrived(gbuf.at[3], ag_recv.at[3])
                ag_copy(3, 2, plus, 0, 2).start()
                arrived(gbuf.at[2], ag_recv.at[2])
                ag_copy(2, 1, minus, 1, 1).start()
            if s == 1:
                arrived(gbuf.at[1], ag_recv.at[1])
                ag_copy(1, 0, plus, 2, 0, gate_cols).start()
                arrived(gbuf.at[0], ag_recv.at[0])
                ag_copy(0, 0, minus, 3, 4, up_cols).start()

        nt = (((1,), (1,)), ((), ()))
        for other in range(2):
            rows = pl.ds(other * feat, feat)
            result = (
                lax.dot_general(wg[rows], gbuf[s, :, :hid], nt, preferred_element_type=F32)
                + lax.dot_general(wu[rows], gbuf[s, :, hid:], nt, preferred_element_type=F32)
                + rterm[s, rows]
            )
            obuf[s, rows] = result.astype(BF16)
            remote(
                obuf.at[s, rows], out_ref.at[:, tile_lanes(s)], d_send.at[s, other], d_recv.at[s, role],
                (before, 2 * y + other),
            ).start()

    for copy in incoming:
        copy.wait_send()
    for copy in exchange:
        copy.wait_send()

    @pl.when(near)
    def _():
        sent(sbuf.at[0, :, low], rs_send.at[0])
        sent(sbuf.at[0, :, high], rs_send.at[3])
        for s in (1, 2):
            sent(sbuf.at[s], rs_send.at[s])
        for s, send in ((3, 0), (3, 1), (2, 2), (1, 3)):
            sent(gbuf.at[s], ag_send.at[send])

    @pl.when(far)
    def _():
        for s in range(4):
            sent(sbuf.at[s], rs_send.at[s])
        sent(gbuf.at[3], ag_send.at[0])
        sent(gbuf.at[2], ag_send.at[1])
        sent(gbuf.at[1, :, gate_cols], ag_send.at[2])
        sent(gbuf.at[0, :, up_cols], ag_send.at[3])

    for s in range(4):
        for other in range(2):
            sent(obuf.at[s, pl.ds(other * feat, feat)], d_send.at[s, other])
            arrived(out_ref.at[:, pl.ds(0, tile)], d_recv.at[s, other])


def shards(upstream, shared_down, shared_gate, shared_up, router_weight, gate_pre, up_pre, gate_grad, gate_scores, expert_ids):
    n_pipe = lax.axis_size("pipe")
    n_chip = lax.axis_size("expert") // 2
    _, tokens, feat = upstream.shape
    rows, hid = gate_pre.shape[1:]
    tile = 2 * rows
    n_experts = router_weight.shape[2]
    top = gate_grad.shape[2]
    args = (
        upstream[0].T, shared_down[0].T, shared_gate[0], shared_up[0], router_weight[0], gate_pre[0], up_pre[0],
        gate_grad[0].T, gate_scores[0].T, expert_ids[0].T,
    )
    vm = pltpu.VMEM
    dma = pltpu.SemaphoreType.DMA
    out = pl.pallas_call(
        functools.partial(kernel, n_pipe, n_chip),
        out_shape=jax.ShapeDtypeStruct((feat, tokens), BF16),
        in_specs=[pl.BlockSpec(memory_space=pl.ANY)] * len(args),
        out_specs=pl.BlockSpec(memory_space=pl.ANY),
        scratch_shapes=[
            vm((4, 2 * feat, tile), BF16),
            vm((2 * feat, hid), BF16),
            vm((2 * feat, hid), BF16),
            vm((2 * feat, hid), BF16),
            vm((2 * feat, n_experts), BF16),
            vm((tile, hid), BF16),
            vm((tile, hid), BF16),
            vm((top, tokens), F32),
            vm((top, tokens), F32),
            vm((top, tokens), jnp.int32),
            vm((tile, hid), F32),
            vm((tile, hid), F32),
            vm((tile, hid), F32),
            vm((4, tile, hid), BF16),
            vm((4, tile, hid), BF16),
            vm((4, tile, 2 * hid), BF16),
            vm((4, 2 * feat, tile), F32),
            vm((4, 2 * feat, tile), BF16),
            dma((9,)), dma((8,)), dma((4, 2)), dma((6,)), dma((6,)),
            dma((4,)), dma((4,)), dma((4,)), dma((5,)), dma((4, 2)), dma((4, 2)),
        ],
        compiler_params=pltpu.CompilerParams(collective_id=0, has_side_effects=True, vmem_limit_bytes=67043328),
    )(*args)
    return out.T[None]


def solution(mesh):
    in_specs = (
        P("pipe", None, "expert"),
        P("pipe", None, "expert"),
        P("pipe", "expert", None),
        P("pipe", "expert", None),
        P("pipe", "expert", None),
        P("pipe", "expert", None),
        P("pipe", "expert", None),
        P("pipe", None, None),
        P("pipe", None, None),
        P("pipe", None, None),
    )
    out_specs = P("pipe", None, "expert")
    return jax.shard_map(shards, mesh=mesh, in_specs=in_specs, out_specs=out_specs, check_vma=False)
```

time: 194 us -> 91.5 us (0.47)
  the two profiles are of different devices: /device:TPU:1 before, /device:TPU:16 now
where the time goes in v1:
time: 91.5 us; the launch traced here: 91.3 us
  Pallas kernels  89.2 us (97%)
  local copies, waits for them, and re-layouts  2.16 us (2%)
    pallas_call x1, Pallas kernels, shards(): pl.pallas_call(functools.partial(kernel, n_pipe, n_chip), out_shape=jax.S...  89.2 us
    unnamed x1, local copies, waits for them, and re-layouts  2.16 us

profile of v1, /device:TPU:16, one launch (start us, length us, event | category | flops | bytes accessed | tf_op | source)
XLA Modules:
  0.0 91.3 jit_solution(12518035893209342822)
XLA Ops:
  0.0 89.2 %shard_map.100 = bf16[448,1024]{1,0:T(8,128)(2,1)} custom-call(bf16[448,1024]{1,0:T(8,128)(2,1)} %bitcast.24, bf16[448,1024]{1,0:T(8,128)(2,1)} %bitcast.25, bf16[448,1024]{1,0:T(8,128)(2,1)} %bitcast.26, bf16[448,1024]{1,0:T(8,128)(2,1)} %bitcast.27, bf16[448,256]{1,0:T(8,128)(2,1)} %bitcast.28, bf16[64,1024]{1,0:T(8,128)(2,1)} %bitcast.29, ...), custom_call_target="tpu_custom_call" | custom-call | tf_op jit(solution)/shard_map/pallas_call | solution.py:259
  89.2 2.2 %copy.12 = bf16[1,1024,448]{1,2,0:T(8,128)(2,1)} copy(bf16[1,1024,448]{1,2,0:T(8,128)(2,1)} %bitcast.23) | data formatting | bytes 1835008

commit v2 on v1

--- a/solution.py
+++ b/solution.py
@@ -12,7 +12,8 @@
 BF16 = jnp.bfloat16
 NEAR = (4, 2, -2, 0)
 FAR = (3, -3, 1, -1)
-ARRIVAL = ((0, 0), (1, 0), (1, 1), (0, 1), (0, 2), (1, 2), (1, 3), (0, 3))
+PARTS = 4
+LEAVING = tuple(k for i in range(PARTS // 2) for k in (i, PARTS // 2 + i))
 
 
 def kernel(
@@ -25,7 +26,6 @@
     feat = up_ref.shape[0]
     tile = pa_ref.shape[0] * 2
     hid = pa_ref.shape[1]
-    half = hid // 2
     p = lax.axis_index("pipe")
     e = lax.axis_index("expert")
     y, c = e // 2, e % 2
@@ -68,9 +68,12 @@
         return pl.ds(pl.multiple_of(lax.rem(y + n_chip + distance, n_chip) * tile, tile), tile)
 
     incoming = []
-    for i, (r, s) in enumerate(ARRIVAL):
-        device = (before, 2 * y + lax.rem(y + r, 2))
-        copy = remote(up_ref.at[:, lanes((NEAR, FAR)[r][s])], up.at[s, mine], a_send.at[i], a_recv.at[s, c], device)
+    for i in range(8):
+        target, slot = i % 2, i // 2
+        distance = jnp.where(lax.rem(target + y, 2) == 0, NEAR[slot], FAR[slot])
+        copy = remote(
+            up_ref.at[:, lanes(distance)], up.at[slot, mine], a_send.at[i], a_recv.at[slot, c], (before, 2 * y + target)
+        )
         copy.start()
         incoming.append(copy)
     exchange = [remote(s, d.at[rows], w_send.at[i], w_recv.at[i], partner) for i, (s, d, rows) in enumerate(wide)]
@@ -117,10 +120,36 @@
 
     have(0)
 
-    def rs_copy(src, slot, device, send, cols=slice(None)):
-        return remote(src.at[:, cols], rbuf.at[slot, :, cols], rs_send.at[send], rs_recv.at[slot], device)
-
-    low, high = pl.ds(0, half), pl.ds(half, half)
+    width, gate_width = hid // PARTS, 2 * hid // PARTS
+
+    def cut(k):
+        return pl.ds(k * width, width)
+
+    def wide_cut(k):
+        return pl.ds(k * gate_width, gate_width)
+
+    def rs_copy(src, slot, device, k):
+        return remote(sbuf.at[src, :, cut(k)], rbuf.at[slot, :, cut(k)], rs_send.at[src, k], rs_recv.at[slot, k], device)
+
+    def rs_arrived(slot, k):
+        arrived(rbuf.at[slot, :, cut(k)], rs_recv.at[slot, k])
+
+    def ag_copy(here, there, device, send, k):
+        return remote(
+            gbuf.at[here, :, wide_cut(k)], gbuf.at[there, :, wide_cut(k)], ag_send.at[send, k], ag_recv.at[there, k], device
+        )
+
+    def ag_arrived(slot, k):
+        arrived(gbuf.at[slot, :, wide_cut(k)], ag_recv.at[slot, k])
+
+    def step(s, k, slots):
+        value = pf[:, cut(k)]
+        for slot in slots:
+            rs_arrived(slot, k)
+            value = value + rbuf[slot, :, cut(k)].astype(F32)
+        return value
+
+    first, second = tuple(range(PARTS // 2)), tuple(range(PARTS // 2, PARTS))
     for s in range(4):
         for other in range(2):
             rows = pl.ds(other * feat, feat)
@@ -129,75 +158,62 @@
 
         @pl.when(near)
         def _(s=s):
-            if s == 0:
-                sbuf[0] = pf[...].astype(BF16)
-                rs_copy(sbuf.at[0], 0, plus, 0, low).start()
-                rs_copy(sbuf.at[0], 1, minus, 3, high).start()
-            elif s < 3:
-                arrived(rbuf.at[s - 1], rs_recv.at[s - 1])
-                sbuf[s] = (pf[...] + rbuf[s - 1].astype(F32)).astype(BF16)
-                rs_copy(sbuf.at[s], s + 1, (plus, minus)[s - 1], s).start()
-            else:
-                arrived(rbuf.at[2], rs_recv.at[2])
-                arrived(rbuf.at[3], rs_recv.at[3])
-                hidden = pf[...] + rbuf[2].astype(F32) + rbuf[3].astype(F32)
-                gbuf[3, :, :hid] = (hidden * c1[...]).astype(BF16)
-                gbuf[3, :, hid:] = (hidden * c2[...]).astype(BF16)
+            for k in range(PARTS):
+                value = step(s, k, ((), (0,), (1,), (2, 3))[s])
+                if s < 3:
+                    sbuf[s, :, cut(k)] = value.astype(BF16)
+                    if s == 0:
+                        rs_copy(0, k // (PARTS // 2), (plus, minus)[k // (PARTS // 2)], k).start()
+                    else:
+                        rs_copy(s, s + 1, (plus, minus)[s - 1], k).start()
+                else:
+                    gbuf[3, :, cut(k)] = (value * c1[:, cut(k)]).astype(BF16)
+                    gbuf[3, :, cut(PARTS + k)] = (value * c2[:, cut(k)]).astype(BF16)
+                    if k % 2 == 1:
+                        for j in (k // 2, PARTS // 2 + k // 2):
+                            ag_copy(3, 3, plus, 0, j).start()
+                            ag_copy(3, 2, minus, 1, j).start()
 
         @pl.when(far)
         def _(s=s):
-            if s < 2:
-                cols = (low, high)[s]
-                arrived(rbuf.at[s, :, cols], rs_recv.at[s])
-                if s == 0:
-                    sbuf[s, :, :half] = (pf[:, :half] + rbuf[s, :, :half].astype(F32)).astype(BF16)
-                    sbuf[s, :, half:] = pf[:, half:].astype(BF16)
-                else:
-                    sbuf[s, :, :half] = pf[:, :half].astype(BF16)
-                    sbuf[s, :, half:] = (pf[:, half:] + rbuf[s, :, half:].astype(F32)).astype(BF16)
-            else:
-                arrived(rbuf.at[s], rs_recv.at[s])
-                sbuf[s] = (pf[...] + rbuf[s].astype(F32)).astype(BF16)
-            rs_copy(sbuf.at[s], s, (plus, minus)[s % 2], s).start()
-
-    def ag_copy(here, there, device, send, recv, cols=slice(None)):
-        return remote(gbuf.at[here, :, cols], gbuf.at[there, :, cols], ag_send.at[send], ag_recv.at[recv], device)
-
-    gate_cols, up_cols = pl.ds(0, hid), pl.ds(hid, hid)
+            for k in second + first if s == 0 else first + second:
+                summed = s >= 2 or k in (first, second)[s]
+                sbuf[s, :, cut(k)] = step(s, k, (s,) if summed else ()).astype(BF16)
+                rs_copy(s, s, (plus, minus)[s % 2], k).start()
 
     have(4)
     have(5)
-
-    @pl.when(near)
-    def _():
-        ag_copy(3, 3, plus, 0, 3).start()
-        ag_copy(3, 2, minus, 1, 2).start()
 
     for s in (3, 2, 1, 0):
 
         @pl.when(near)
         def _(s=s):
             if s == 2:
-                arrived(gbuf.at[2], ag_recv.at[2])
-                ag_copy(2, 1, plus, 2, 1).start()
-                arrived(gbuf.at[1], ag_recv.at[1])
-                ag_copy(1, 0, minus, 3, 0).start()
+                for k in LEAVING:
+                    ag_arrived(2, k)
+                    ag_copy(2, 1, plus, 2, k).start()
+                    ag_arrived(1, k)
+                    ag_copy(1, 0, minus, 3, k).start()
             if s == 0:
-                arrived(gbuf.at[0, :, gate_cols], ag_recv.at[0])
-                arrived(gbuf.at[0, :, up_cols], ag_recv.at[4])
+                for k in LEAVING:
+                    ag_arrived(0, k)
 
         @pl.when(far)
         def _(s=s):
             if s == 3:
-                arrived(gbuf.at[3], ag_recv.at[3])
-                ag_copy(3, 2, plus, 0, 2).start()
-                arrived(gbuf.at[2], ag_recv.at[2])
-                ag_copy(2, 1, minus, 1, 1).start()
+                for k in LEAVING:
+                    ag_arrived(3, k)
+                    ag_copy(3, 2, plus, 0, k).start()
+                    ag_arrived(2, k)
+                    ag_copy(2, 1, minus, 1, k).start()
             if s == 1:
-                arrived(gbuf.at[1], ag_recv.at[1])
-                ag_copy(1, 0, plus, 2, 0, gate_cols).start()
-                arrived(gbuf.at[0], ag_recv.at[0])
-                ag_copy(0, 0, minus, 3, 4, up_cols).start()
+                for k in LEAVING:
+                    ag_arrived(1, k)
+                    if k in first:
+                        ag_copy(1, 0, plus, 2, k).start()
+                    ag_arrived(0, k)
+                    if k in second:
+                        ag_copy(0, 0, minus, 3, k).start()
 
         nt = (((1,), (1,)), ((), ()))
         for other in range(2):
@@ -218,23 +234,28 @@
     for copy in exchange:
         copy.wait_send()
 
-    @pl.when(near)
-    def _():
-        sent(sbuf.at[0, :, low], rs_send.at[0])
-        sent(sbuf.at[0, :, high], rs_send.at[3])
-        for s in (1, 2):
-            sent(sbuf.at[s], rs_send.at[s])
-        for s, send in ((3, 0), (3, 1), (2, 2), (1, 3)):
-            sent(gbuf.at[s], ag_send.at[send])
-
-    @pl.when(far)
-    def _():
-        for s in range(4):
-            sent(sbuf.at[s], rs_send.at[s])
-        sent(gbuf.at[3], ag_send.at[0])
-        sent(gbuf.at[2], ag_send.at[1])
-        sent(gbuf.at[1, :, gate_cols], ag_send.at[2])
-        sent(gbuf.at[0, :, up_cols], ag_send.at[3])
+    def ag_sent(slot, send, k):
+        sent(gbuf.at[slot, :, wide_cut(k)], ag_send.at[send, k])
+
+    for k in range(PARTS):
+
+        @pl.when(near)
+        def _(k=k):
+            for s in range(3):
+                sent(sbuf.at[s, :, cut(k)], rs_send.at[s, k])
+            for slot, send in ((3, 0), (3, 1), (2, 2), (1, 3)):
+                ag_sent(slot, send, k)
+
+        @pl.when(far)
+        def _(k=k):
+            for s in range(4):
+                sent(sbuf.at[s, :, cut(k)], rs_send.at[s, k])
+            ag_sent(3, 0, k)
+            ag_sent(2, 1, k)
+            if k in first:
+                ag_sent(1, 2, k)
+            else:
+                ag_sent(0, 3, k)
 
     for s in range(4):
         for other in range(2):
@@ -281,7 +302,7 @@
             vm((4, 2 * feat, tile), F32),
             vm((4, 2 * feat, tile), BF16),
             dma((9,)), dma((8,)), dma((4, 2)), dma((6,)), dma((6,)),
-            dma((4,)), dma((4,)), dma((4,)), dma((5,)), dma((4, 2)), dma((4, 2)),
+            dma((4, PARTS)), dma((4, PARTS)), dma((4, PARTS)), dma((4, PARTS)), dma((4, 2)), dma((4, 2)),
         ],
         compiler_params=pltpu.CompilerParams(collective_id=0, has_side_effects=True, vmem_limit_bytes=67043328),
     )(*args)

time: 91.5 us -> 73.3 us (0.80)
  the two profiles are of different devices: /device:TPU:16 before, /device:TPU:8 now
where the time goes in v2:
time: 73.3 us; the launch traced here: 73.2 us
  Pallas kernels  71 us (97%)
  local copies, waits for them, and re-layouts  2.16 us (3%)
    pallas_call x1, Pallas kernels, shards(): pl.pallas_call(functools.partial(kernel, n_pipe, n_chip), out_shape=jax.S...  71 us
    unnamed x1, local copies, waits for them, and re-layouts  2.16 us

profile of v2, /device:TPU:8, one launch (start us, length us, event | category | flops | bytes accessed | tf_op | source)
XLA Modules:
  0.0 73.2 jit_solution(13588748744982239599)
XLA Ops:
  0.0 71.0 %shard_map.100 = bf16[448,1024]{1,0:T(8,128)(2,1)} custom-call(bf16[448,1024]{1,0:T(8,128)(2,1)} %bitcast.24, bf16[448,1024]{1,0:T(8,128)(2,1)} %bitcast.25, bf16[448,1024]{1,0:T(8,128)(2,1)} %bitcast.26, bf16[448,1024]{1,0:T(8,128)(2,1)} %bitcast.27, bf16[448,256]{1,0:T(8,128)(2,1)} %bitcast.28, bf16[64,1024]{1,0:T(8,128)(2,1)} %bitcast.29, ...), custom_call_target="tpu_custom_call" | custom-call | tf_op jit(solution)/shard_map/pallas_call | solution.py:280
  71.0 2.2 %copy.12 = bf16[1,1024,448]{1,2,0:T(8,128)(2,1)} copy(bf16[1,1024,448]{1,2,0:T(8,128)(2,1)} %bitcast.23) | data formatting | bytes 1835008

commit v3 on v2

--- a/solution.py
+++ b/solution.py
@@ -12,7 +12,7 @@
 BF16 = jnp.bfloat16
 NEAR = (4, 2, -2, 0)
 FAR = (3, -3, 1, -1)
-PARTS = 4
+PARTS = 8
 LEAVING = tuple(k for i in range(PARTS // 2) for k in (i, PARTS // 2 + i))
 
 
@@ -77,7 +77,7 @@
         copy.start()
         incoming.append(copy)
     exchange = [remote(s, d.at[rows], w_send.at[i], w_recv.at[i], partner) for i, (s, d, rows) in enumerate(wide)]
-    for copy in exchange:
+    for copy in exchange[:4]:
         copy.start()
 
     theirs = pl.ds(pl.multiple_of((1 - c) * feat, feat), feat)
@@ -92,31 +92,33 @@
         distance = jnp.where(near, NEAR[s], FAR[s])
         return pl.ds(pl.multiple_of(lax.rem(y + n_chip + distance, n_chip) * tile, tile), tile)
 
-    for i in range(3):
-        local[i].wait()
-    have(1)
-    for s in range(4):
-        where = tile_lanes(s)
-        grad, score, chosen = gg[:, where], sc[:, where], ids[:, where]
-        total = jnp.sum(score, axis=0, keepdims=True)
-        mixed = jnp.sum(grad * score, axis=0, keepdims=True)
-        logit = 2.5 * (grad - mixed / total) / total * score * (1.0 - score)
-        n_experts = wr.shape[1]
-        rows = lax.broadcasted_iota(jnp.int32, (n_experts, tile), 0)
-        dense = jnp.zeros((n_experts, tile), F32)
-        for k in range(grad.shape[0]):
-            dense = dense + jnp.where(chosen[k : k + 1] == rows, logit[k : k + 1], 0.0)
-        rterm[s] = jnp.dot(wr[...], dense.astype(BF16), preferred_element_type=F32)
-
-    have(2)
-    have(3)
-
-    @pl.when(near)
-    def _():
-        a, b = pa[...].astype(F32), pb[...].astype(F32)
-        sigma = 1.0 / (1.0 + jnp.exp(-a))
-        c1[...] = b * sigma * (1.0 + a * (1.0 - sigma))
-        c2[...] = a * sigma
+    def router_term():
+        for i in range(3):
+            local[i].wait()
+        have(1)
+        for s in range(4):
+            where = tile_lanes(s)
+            grad, score, chosen = gg[:, where], sc[:, where], ids[:, where]
+            total = jnp.sum(score, axis=0, keepdims=True)
+            mixed = jnp.sum(grad * score, axis=0, keepdims=True)
+            logit = 2.5 * (grad - mixed / total) / total * score * (1.0 - score)
+            n_experts = wr.shape[1]
+            rows = lax.broadcasted_iota(jnp.int32, (n_experts, tile), 0)
+            dense = jnp.zeros((n_experts, tile), F32)
+            for k in range(grad.shape[0]):
+                dense = dense + jnp.where(chosen[k : k + 1] == rows, logit[k : k + 1], 0.0)
+            rterm[s] = jnp.dot(wr[...], dense.astype(BF16), preferred_element_type=F32)
+
+    def coefficients():
+        have(2)
+        have(3)
+
+        @pl.when(near)
+        def _():
+            a, b = pa[...].astype(F32), pb[...].astype(F32)
+            sigma = 1.0 / (1.0 + jnp.exp(-a))
+            c1[...] = b * sigma * (1.0 + a * (1.0 - sigma))
+            c2[...] = a * sigma
 
     have(0)
 
@@ -180,6 +182,13 @@
                 summed = s >= 2 or k in (first, second)[s]
                 sbuf[s, :, cut(k)] = step(s, k, (s,) if summed else ()).astype(BF16)
                 rs_copy(s, s, (plus, minus)[s % 2], k).start()
+
+        if s == 0:
+            for copy in exchange[4:]:
+                copy.start()
+            router_term()
+        if s == 1:
+            coefficients()
 
     have(4)
     have(5)

time: 73.3 us -> 71.1 us (0.970)
  Pallas kernels: 71 us -> 68.8 us
    pallas_call x1, Pallas kernels: 71 us -> 68.8 us  [shards(): pl.pallas_call(functools.partial(kernel, n_pipe, n_chip), out_shape=jax.S...]
where the time goes in v3:
time: 71.1 us; the launch traced here: 70.9 us
  Pallas kernels  68.8 us (97%)
  local copies, waits for them, and re-layouts  2.16 us (3%)
    pallas_call x1, Pallas kernels, shards(): pl.pallas_call(functools.partial(kernel, n_pipe, n_chip), out_shape=jax.S...  68.8 us
    unnamed x1, local copies, waits for them, and re-layouts  2.16 us

profile of v3, /device:TPU:8, one launch (start us, length us, event | category | flops | bytes accessed | tf_op | source)
XLA Modules:
  0.0 70.9 jit_solution(8039478929478406951)
XLA Ops:
  0.0 68.8 %shard_map.100 = bf16[448,1024]{1,0:T(8,128)(2,1)} custom-call(bf16[448,1024]{1,0:T(8,128)(2,1)} %bitcast.24, bf16[448,1024]{1,0:T(8,128)(2,1)} %bitcast.25, bf16[448,1024]{1,0:T(8,128)(2,1)} %bitcast.26, bf16[448,1024]{1,0:T(8,128)(2,1)} %bitcast.27, bf16[448,256]{1,0:T(8,128)(2,1)} %bitcast.28, bf16[64,1024]{1,0:T(8,128)(2,1)} %bitcast.29, ...), custom_call_target="tpu_custom_call" | custom-call | tf_op jit(solution)/shard_map/pallas_call | solution.py:289
  68.8 2.2 %copy.12 = bf16[1,1024,448]{1,2,0:T(8,128)(2,1)} copy(bf16[1,1024,448]{1,2,0:T(8,128)(2,1)} %bitcast.23) | data formatting | bytes 1835008
